TPU v7x, 32 devices: a whole 2x2x4 slice. The times are simulated.
32 devices in a mesh: dp: 8 (over z, y), tensor: 4 (over x, core).
Axes of the slice: x: 2, y: 2, z: 4, core: 2. Of those that a mesh axis runs over, the one named last changes fastest.
Arguments:
- tokens: bfloat16 [4096, 1024], P(('dp', 'tensor')), may hold values from -6 to 6
- segment_ids: int32 [4096], P('dp'), may hold values from 0 to 31, never falling along the last dimension, each value on 1 to 256 neighbouring positions
- norm_gain_mixer: bfloat16 [1024], P('dp'), may hold values from 0.5 to 1.5
- query_weight: bfloat16 [1024, 1024], P('dp', 'tensor'), may hold values from -0.1875 to 0.1875
- key_weight: bfloat16 [1024, 1024], P('dp', 'tensor'), may hold values from -0.1875 to 0.1875
- value_weight: bfloat16 [1024, 2048], P('dp', 'tensor'), may hold values from -0.1875 to 0.1875
- gate_weight: bfloat16 [1024, 2048], P('dp', 'tensor'), may hold values from -0.1875 to 0.1875
- alpha_weight: bfloat16 [1024, 8], P('dp', 'tensor'), may hold values from -0.1875 to 0.1875
- beta_weight: bfloat16 [1024, 8], P('dp', 'tensor'), may hold values from -0.1875 to 0.1875
- conv_query: bfloat16 [4, 8, 128], P(None, 'tensor', 'dp'), may hold values from -3 to 3
- conv_key: bfloat16 [4, 8, 128], P(None, 'tensor', 'dp'), may hold values from -3 to 3
- conv_value: bfloat16 [4, 8, 256], P(None, 'tensor', 'dp'), may hold values from -3 to 3
- decay_log: float32 [8], P('tensor'), may hold values from 0 to 2.7725887
- decay_bias: float32 [8], P('tensor'), may hold values from -6.9073 to -2.2521, as said below
- output_gain: bfloat16 [8, 256], P('tensor', 'dp'), may hold values from 0.5 to 1.5
- output_weight: bfloat16 [2048, 1024], P('tensor', 'dp'), may hold values from -0.125 to 0.125
- norm_gain_ffn: bfloat16 [1024], P('dp'), may hold values from 0.5 to 1.5
- ffn_gate: bfloat16 [1024, 2816], P('dp', 'tensor'), may hold values from -0.1875 to 0.1875
- ffn_up: bfloat16 [1024, 2816], P('dp', 'tensor'), may hold values from -0.1875 to 0.1875
- ffn_down: bfloat16 [2816, 1024], P('tensor', 'dp'), may hold values from -0.109375 to 0.109375
- grad_block: bfloat16 [4096, 1024], P(('dp', 'tensor')), may hold values from -6 to 6
Outputs:
- block_output: bfloat16 [4096, 1024], P(('dp', 'tensor'))
- tokens_grad: float32 [4096, 1024], P(('dp', 'tensor'))
- norm_gain_mixer_grad: float32 [1024], P('dp')
- query_weight_grad: float32 [1024, 1024], P('dp', 'tensor')
- key_weight_grad: float32 [1024, 1024], P('dp', 'tensor')
- value_weight_grad: float32 [1024, 2048], P('dp', 'tensor')
- gate_weight_grad: float32 [1024, 2048], P('dp', 'tensor')
- alpha_weight_grad: float32 [1024, 8], P('dp', 'tensor')
- beta_weight_grad: float32 [1024, 8], P('dp', 'tensor')
- conv_query_grad: float32 [4, 8, 128], P(None, 'tensor', 'dp')
- conv_key_grad: float32 [4, 8, 128], P(None, 'tensor', 'dp')
- conv_value_grad: float32 [4, 8, 256], P(None, 'tensor', 'dp')
- decay_log_grad: float32 [8], P('tensor')
- decay_bias_grad: float32 [8], P('tensor')
- output_gain_grad: float32 [8, 256], P('tensor', 'dp')
- output_weight_grad: float32 [2048, 1024], P('tensor', 'dp')
- norm_gain_ffn_grad: float32 [1024], P('dp')
- ffn_gate_grad: float32 [1024, 2816], P('dp', 'tensor')
- ffn_up_grad: float32 [1024, 2816], P('dp', 'tensor')
- ffn_down_grad: float32 [2816, 1024], P('tensor', 'dp')
Inputs may be any that keep to these rules, and one draw needn't show every extreme that they name: `segment_ids`: segment ids never fall along the tokens; a document has at most 256 tokens, and one has exactly that many. `decay_bias`: each entry is log(exp(dt) - 1) for a step size dt between 0.001 and 0.1.
All inputs are finite; a program needn't handle non-finite values.
Results may differ from a plain program's by a relative error of at most 0.013.
Values may be sent and summed in bfloat16 or wider, within the bound.
No kernel may reach another device: no remote copies, remote signals or barrier semaphores. Data moves between devices by JAX's collectives and lax.ppermute only.
A program may use at most 192 MiB of HBM per device.

v0:
```python
from functools import partial

import jax
import jax.numpy as jnp
from jax import lax
from jax.sharding import PartitionSpec as P

GROUP = 64
LEN = 512


highest = lax.Precision.HIGHEST
eps_norm = 1e-06
eps_output = 1e-05


def times_transposed(left, right):
    return lax.dot_general(
        left, right, (((1,), (1,)), ((), ())), preferred_element_type=jnp.float32
    )


def transposed_times(left, right):
    return lax.dot_general(
        left, right, (((0,), (0,)), ((), ())), preferred_element_type=jnp.float32
    )


def short_conv(values, kernel, segment):
    length = values.shape[0]
    result = kernel[0] * values
    for offset in range(1, kernel.shape[0]):
        before = jnp.concatenate(
            [jnp.zeros((offset, values.shape[1]), values.dtype), values[: length - offset]], axis=0
        )
        earlier = jnp.concatenate(
            [jnp.full((offset,), -1, jnp.int32), segment[: length - offset]], axis=0
        )
        same_doc = (segment == earlier).astype(values.dtype)[:, None]
        result = result + kernel[offset] * before * same_doc
    return result


def delta_block(carry, pieces):
    state, last_segment = carry
    query, key, value, beta, logdecay, segment = pieces
    width = segment.shape[0]
    cumul = jnp.cumsum(logdecay, axis=1)
    row_index = lax.broadcasted_iota(jnp.int32, (width, width), 0)
    col_index = lax.broadcasted_iota(jnp.int32, (width, width), 1)
    within = (segment[:, None] == segment[None, :]) & (row_index >= col_index)
    strict = within & (row_index > col_index)
    spread = cumul[:, :, None] - cumul[:, None, :]
    decay = jnp.where(within[None], jnp.exp(jnp.where(within[None], spread, 0.0)), 0.0)
    carried = jnp.where((segment == last_segment)[None, :], jnp.exp(cumul), 0.0)
    keykey = jnp.einsum("hcd,hed->hce", key, key, precision=highest)
    lower = jnp.where(strict[None], beta[:, :, None] * decay * keykey, 0.0)
    system = lower + jnp.eye(width, dtype=query.dtype)[None]
    known = jnp.einsum("hcd,hdf->hcf", key, state, precision=highest)
    target = beta[:, :, None] * (value - carried[:, :, None] * known)
    update = lax.linalg.triangular_solve(
        system, target, left_side=True, lower=True, unit_diagonal=True
    )
    scores = jnp.einsum("hcd,hed->hce", query, key, precision=highest) * decay
    output = carried[:, :, None] * jnp.einsum("hcd,hdf->hcf", query, state, precision=highest)
    output = output + jnp.einsum("hce,hef->hcf", scores, update, precision=highest)
    weighted = decay[:, -1, :][:, :, None] * key
    state = carried[:, -1][:, None, None] * state + jnp.einsum(
        "hcd,hcf->hdf", weighted, update, precision=highest
    )
    return ((state, segment[-1]), output)


def mixer_core(
    segment,
    proj_q,
    proj_k,
    proj_v,
    proj_g,
    proj_a,
    proj_b,
    conv_q,
    conv_k,
    conv_v,
    decay_log,
    decay_bias,
    output_gain,
):
    length = proj_q.shape[0]
    heads = decay_log.shape[0]
    query = jax.nn.silu(short_conv(proj_q, conv_q.reshape(conv_q.shape[0], -1), segment)).reshape(
        length, heads, -1
    )
    key = jax.nn.silu(short_conv(proj_k, conv_k.reshape(conv_k.shape[0], -1), segment)).reshape(
        length, heads, -1
    )
    value = jax.nn.silu(short_conv(proj_v, conv_v.reshape(conv_v.shape[0], -1), segment)).reshape(
        length, heads, -1
    )
    query = (
        query
        * lax.rsqrt(jnp.sum(query * query, axis=-1, keepdims=True) + eps_norm)
        * query.shape[-1] ** (-0.5)
    )
    key = key * lax.rsqrt(jnp.sum(key * key, axis=-1, keepdims=True) + eps_norm)
    beta = jax.nn.sigmoid(proj_b)
    logdecay = -jnp.exp(decay_log) * jax.nn.softplus(proj_a + decay_bias)
    blocks = length // GROUP

    def arrange(tensor):
        return jnp.moveaxis(tensor.reshape(blocks, GROUP, heads, -1), 2, 1)

    def arrange_gate(tensor):
        return jnp.moveaxis(tensor.reshape(blocks, GROUP, heads), 2, 1)

    initial = (
        jnp.zeros((heads, query.shape[-1], value.shape[-1]), query.dtype),
        jnp.array(-1, jnp.int32),
    )
    final, output = lax.scan(
        delta_block,
        initial,
        (
            arrange(query),
            arrange(key),
            arrange(value),
            arrange_gate(beta),
            arrange_gate(logdecay),
            segment.reshape(blocks, GROUP),
        ),
    )
    output = jnp.moveaxis(output, 1, 2).reshape(length, heads, -1)
    scale = lax.rsqrt(jnp.mean(output * output, axis=-1, keepdims=True) + eps_output)
    gated = output * scale * output_gain * jax.nn.silu(proj_g.reshape(length, heads, -1))
    return gated.reshape(length, -1)


def sequence_core(
    segment,
    proj_q,
    proj_k,
    proj_v,
    proj_g,
    proj_a,
    proj_b,
    conv_q,
    conv_k,
    conv_v,
    decay_log,
    decay_bias,
    output_gain,
):
    sequences = segment.shape[0] // LEN
    split = tuple(
        (
            piece.reshape(sequences, LEN, piece.shape[-1])
            for piece in (proj_q, proj_k, proj_v, proj_g, proj_a, proj_b)
        )
    )
    shared = (conv_q, conv_k, conv_v, decay_log, decay_bias, output_gain)
    mapped = jax.vmap(
        mixer_core, in_axes=(0, 0, 0, 0, 0, 0, 0, None, None, None, None, None, None)
    )(segment.reshape(sequences, LEN), *split + shared)
    return mapped.reshape(sequences * LEN, -1)


def row_scale(values):
    return lax.rsqrt(jnp.mean(values * values, axis=-1, keepdims=True) + eps_norm)


def norm_back(grad, normed, scale):
    return scale * (grad - normed * jnp.mean(grad * normed, axis=-1, keepdims=True))


def per_device(
    tokens,
    segment_ids,
    norm_gain_mixer,
    query_weight,
    key_weight,
    value_weight,
    gate_weight,
    alpha_weight,
    beta_weight,
    conv_query,
    conv_key,
    conv_value,
    decay_log,
    decay_bias,
    output_gain,
    output_weight,
    norm_gain_ffn,
    ffn_gate,
    ffn_up,
    ffn_down,
    grad_block,
):
    gathered = (
        lax.all_gather(norm_gain_mixer, "dp", axis=0, tiled=True),
        lax.all_gather(query_weight, "dp", axis=0, tiled=True),
        lax.all_gather(key_weight, "dp", axis=0, tiled=True),
        lax.all_gather(value_weight, "dp", axis=0, tiled=True),
        lax.all_gather(gate_weight, "dp", axis=0, tiled=True),
        lax.all_gather(alpha_weight, "dp", axis=0, tiled=True),
        lax.all_gather(beta_weight, "dp", axis=0, tiled=True),
        lax.all_gather(conv_query, "dp", axis=2, tiled=True),
        lax.all_gather(conv_key, "dp", axis=2, tiled=True),
        lax.all_gather(conv_value, "dp", axis=2, tiled=True),
        lax.all_gather(output_gain, "dp", axis=1, tiled=True),
        lax.all_gather(output_weight, "dp", axis=1, tiled=True),
        lax.all_gather(norm_gain_ffn, "dp", axis=0, tiled=True),
        lax.all_gather(ffn_gate, "dp", axis=0, tiled=True),
        lax.all_gather(ffn_up, "dp", axis=0, tiled=True),
        lax.all_gather(ffn_down, "dp", axis=1, tiled=True),
    )
    (
        gain_mix_all,
        query_all,
        key_all,
        value_all,
        gate_all,
        alpha_all,
        beta_all,
        convq_all,
        convk_all,
        convv_all,
        outgain_all,
        outweight_all,
        gain_ffn_all,
        ffngate_all,
        ffnup_all,
        ffndown_all,
    ) = gathered
    local_rows = tokens.shape[0]
    resid_in = tokens.astype(jnp.float32)
    mixer_rms = row_scale(resid_in)
    mixer_norm = resid_in * mixer_rms
    mixer_in = (mixer_norm * gain_mix_all.astype(jnp.float32)).astype(jnp.bfloat16)
    mixer_full, grad_full = (
        lax.all_gather(mixer_in, "tensor", axis=0, tiled=True),
        lax.all_gather(grad_block, "tensor", axis=0, tiled=True),
    )
    forward_weights = (query_all, key_all, value_all, gate_all, alpha_all, beta_all)
    projected = tuple(
        (
            jnp.dot(mixer_full, weight, preferred_element_type=jnp.float32)
            for weight in forward_weights
        )
    )
    primals = projected + (
        convq_all.astype(jnp.float32),
        convk_all.astype(jnp.float32),
        convv_all.astype(jnp.float32),
        decay_log,
        decay_bias,
        outgain_all.astype(jnp.float32),
    )
    gated, pullback = jax.vjp(partial(sequence_core, segment_ids), *primals)
    out_gated = gated.astype(jnp.bfloat16)
    mixer_out = lax.psum_scatter(
        jnp.dot(out_gated, outweight_all, preferred_element_type=jnp.float32),
        "tensor",
        scatter_dimension=0,
        tiled=True,
    )
    resid = resid_in + mixer_out
    ffn_rms = row_scale(resid)
    ffn_norm = resid * ffn_rms
    ffn_in = (ffn_norm * gain_ffn_all.astype(jnp.float32)).astype(jnp.bfloat16)
    ffn_full = lax.all_gather(ffn_in, "tensor", axis=0, tiled=True)
    gate_pre = jnp.dot(ffn_full, ffngate_all, preferred_element_type=jnp.float32)
    up_pre = jnp.dot(ffn_full, ffnup_all, preferred_element_type=jnp.float32)
    hidden = (jax.nn.silu(gate_pre) * up_pre).astype(jnp.bfloat16)
    ffn_out = lax.psum_scatter(
        jnp.dot(hidden, ffndown_all, preferred_element_type=jnp.float32).astype(jnp.bfloat16),
        "tensor",
        scatter_dimension=0,
        tiled=True,
    ).astype(jnp.float32)
    block_output = (resid + ffn_out).astype(jnp.bfloat16)
    (
        gain_mix_back,
        query_back,
        key_back,
        value_back,
        gate_back,
        alpha_back,
        beta_back,
        convq_back,
        convk_back,
        convv_back,
        outgain_back,
        outweight_back,
        gain_ffn_back,
        ffngate_back,
        ffnup_back,
        ffndown_back,
    ) = gathered
    d_hidden = times_transposed(grad_full, ffndown_back)
    sigma = jax.nn.sigmoid(gate_pre)
    d_gate = (d_hidden * up_pre * sigma * (1.0 + gate_pre * (1.0 - sigma))).astype(jnp.bfloat16)
    d_up = (d_hidden * jax.nn.silu(gate_pre)).astype(jnp.bfloat16)
    down_grad = transposed_times(hidden, grad_full)
    fgate_grad = transposed_times(ffn_full, d_gate)
    fup_grad = transposed_times(ffn_full, d_up)
    d_ffn_in = lax.psum_scatter(
        times_transposed(d_gate, ffngate_back) + times_transposed(d_up, ffnup_back),
        "tensor",
        scatter_dimension=0,
        tiled=True,
    )
    ffn_gain_part = jnp.sum(d_ffn_in * ffn_norm, axis=0)
    d_resid = grad_block.astype(jnp.float32) + norm_back(
        d_ffn_in * gain_ffn_back.astype(jnp.float32), ffn_norm, ffn_rms
    )
    d_mix = d_resid.astype(jnp.bfloat16)
    d_mix_full = lax.all_gather(d_mix, "tensor", axis=0, tiled=True)
    d_gated = times_transposed(d_mix_full, outweight_back)
    outweight_grad = transposed_times(out_gated, d_mix_full)
    pulled = pullback(d_gated)
    rounded = [piece.astype(jnp.bfloat16) for piece in pulled[:6]]
    proj_grads = [transposed_times(mixer_full, piece) for piece in rounded]
    backward_weights = (query_back, key_back, value_back, gate_back, alpha_back, beta_back)
    summed = jnp.zeros((local_rows * lax.axis_size("tensor"), query_back.shape[0]), jnp.float32)
    for piece, weight in zip(rounded, backward_weights):
        summed = summed + times_transposed(piece, weight)
    d_mixer_in = lax.psum_scatter(
        summed.astype(jnp.bfloat16), "tensor", scatter_dimension=0, tiled=True
    ).astype(jnp.float32)
    mix_gain_part = jnp.sum(d_mixer_in * mixer_norm, axis=0)
    tokens_grad = d_resid + norm_back(
        d_mixer_in * gain_mix_back.astype(jnp.float32), mixer_norm, mixer_rms
    )
    (
        query_owned,
        key_owned,
        value_owned,
        gate_owned,
        alpha_owned,
        beta_owned,
        convq_owned,
        convk_owned,
        convv_owned,
        ogain_owned,
        oweight_owned,
        fgate_owned,
        fup_owned,
        fdown_owned,
    ) = (
        lax.psum_scatter(proj_grads[0], "dp", scatter_dimension=0, tiled=True),
        lax.psum_scatter(proj_grads[1], "dp", scatter_dimension=0, tiled=True),
        lax.psum_scatter(proj_grads[2], "dp", scatter_dimension=0, tiled=True),
        lax.psum_scatter(proj_grads[3], "dp", scatter_dimension=0, tiled=True),
        lax.psum_scatter(proj_grads[4], "dp", scatter_dimension=0, tiled=True),
        lax.psum_scatter(proj_grads[5], "dp", scatter_dimension=0, tiled=True),
        lax.psum_scatter(pulled[6], "dp", scatter_dimension=2, tiled=True),
        lax.psum_scatter(pulled[7], "dp", scatter_dimension=2, tiled=True),
        lax.psum_scatter(pulled[8], "dp", scatter_dimension=2, tiled=True),
        lax.psum_scatter(pulled[11], "dp", scatter_dimension=1, tiled=True),
        lax.psum_scatter(outweight_grad, "dp", scatter_dimension=1, tiled=True),
        lax.psum_scatter(fgate_grad, "dp", scatter_dimension=0, tiled=True),
        lax.psum_scatter(fup_grad, "dp", scatter_dimension=0, tiled=True),
        lax.psum_scatter(down_grad, "dp", scatter_dimension=1, tiled=True),
    )
    heads_local = decay_log.shape[0]
    head_start = lax.axis_index("tensor") * heads_local
    heads_total = heads_local * lax.axis_size("tensor")

    def spread_heads(part):
        return lax.dynamic_update_slice_in_dim(
            jnp.zeros((heads_total,), jnp.float32), part, head_start, 0
        )

    summed_small = lax.psum(
        (mix_gain_part, ffn_gain_part, spread_heads(pulled[9]), spread_heads(pulled[10])),
        ("dp", "tensor"),
    )
    gain_piece = norm_gain_mixer.shape[0]
    gain_start = lax.axis_index("dp") * gain_piece
    mix_gain_grad = lax.dynamic_slice_in_dim(summed_small[0], gain_start, gain_piece, 0)
    ffn_gain_grad = lax.dynamic_slice_in_dim(summed_small[1], gain_start, gain_piece, 0)
    decay_log_grad = lax.dynamic_slice_in_dim(summed_small[2], head_start, heads_local, 0)
    decay_bias_grad = lax.dynamic_slice_in_dim(summed_small[3], head_start, heads_local, 0)
    return (
        block_output,
        tokens_grad,
        mix_gain_grad,
        query_owned,
        key_owned,
        value_owned,
        gate_owned,
        alpha_owned,
        beta_owned,
        convq_owned,
        convk_owned,
        convv_owned,
        decay_log_grad,
        decay_bias_grad,
        ogain_owned,
        oweight_owned,
        ffn_gain_grad,
        fgate_owned,
        fup_owned,
        fdown_owned,
    )


def solution(mesh):
    placed = (
        P(("dp", "tensor"), None),
        P("dp"),
        P("dp"),
        P("dp", "tensor"),
        P("dp", "tensor"),
        P("dp", "tensor"),
        P("dp", "tensor"),
        P("dp", "tensor"),
        P("dp", "tensor"),
        P(None, "tensor", "dp"),
        P(None, "tensor", "dp"),
        P(None, "tensor", "dp"),
        P("tensor"),
        P("tensor"),
        P("tensor", "dp"),
        P("tensor", "dp"),
        P("dp"),
        P("dp", "tensor"),
        P("dp", "tensor"),
        P("tensor", "dp"),
        P(("dp", "tensor"), None),
    )
    return jax.shard_map(
        per_device,
        mesh=mesh,
        in_specs=placed,
        out_specs=(
            P(("dp", "tensor"), None),
            P(("dp", "tensor"), None),
            P("dp"),
            P("dp", "tensor"),
            P("dp", "tensor"),
            P("dp", "tensor"),
            P("dp", "tensor"),
            P("dp", "tensor"),
            P("dp", "tensor"),
            P(None, "tensor", "dp"),
            P(None, "tensor", "dp"),
            P(None, "tensor", "dp"),
            P("tensor"),
            P("tensor"),
            P("tensor", "dp"),
            P("tensor", "dp"),
            P("dp"),
            P("dp", "tensor"),
            P("dp", "tensor"),
            P("tensor", "dp"),
        ),
        check_vma=False,
    )
```

profile of v0, /device:TPU:0, one launch (start us, length us, event | category | flops | bytes accessed | tf_op | source)
XLA Modules:
  0.0 2360.3 jit_solution(5935738485769750793)
XLA Ops:
  7.3 22.5 all-gather
  34.9 32.0 %all_gather.69 = bf16[1024,256]{1,0:T(8,128)(2,1)S(1)} all-gather(bf16[128,256]{1,0:T(8,128)(2,1)} %param.28), channel_id=1, replica_groups=mesh['dp'=8,'tensor'=4] {'dp'}, dimensions={0}, use_global_device_ids=true | all-gather | bytes 589824 | tf_op jit(solution)/shard_map/all_gather | solution.py:200
  67.0 32.6 %all_gather.64 = bf16[1024,256]{1,0:T(8,128)(2,1)S(1)} all-gather(bf16[128,256]{1,0:T(8,128)(2,1)S(1)} %copy-done.48), channel_id=1, replica_groups=mesh['dp'=8,'tensor'=4] {'dp'}, dimensions={0}, use_global_device_ids=true | all-gather | bytes 589824 | tf_op jit(solution)/shard_map/all_gather | solution.py:201
  99.7 30.6 %all_gather.63 = bf16[4,2,128]{0,1,2:T(2,128)(2,1)S(1)} all-gather(bf16[4,2,16]{0,1,2:T(2,128)(2,1)S(1)} %copy.228), channel_id=1, replica_groups=mesh['dp'=8,'tensor'=4] {'dp'}, dimensions={2}, use_global_device_ids=true | all-gather | bytes 2304 | tf_op jit(solution)/shard_map/all_gather | solution.py:207
  130.8 30.6 %all_gather.68 = bf16[4,2,128]{0,1,2:T(2,128)(2,1)S(1)} all-gather(bf16[4,2,16]{0,1,2:T(2,128)(2,1)S(1)} %copy.242), channel_id=1, replica_groups=mesh['dp'=8,'tensor'=4] {'dp'}, dimensions={2}, use_global_device_ids=true | all-gather | bytes 2304 | tf_op jit(solution)/shard_map/all_gather | solution.py:206
  162.5 30.7 %all_gather.66 = bf16[4,2,256]{0,1,2:T(2,128)(2,1)S(1)} all-gather(bf16[4,2,32]{0,1,2:T(2,128)(2,1)S(1)} %copy.236), channel_id=1, replica_groups=mesh['dp'=8,'tensor'=4] {'dp'}, dimensions={2}, use_global_device_ids=true | all-gather | bytes 4608 | tf_op jit(solution)/shard_map/all_gather | solution.py:208
  194.3 16.3 all_gather.62
  210.6 18.2 all_gather.65
  277.5 325.5 %while.91 = (s32[]{:T(128)}, f32[1,2,128,256]{3,2,1,0:T(8,128)S(1)}, s32[1]{0:T(128)}, f32[8,1,2,64,256]{4,3,2,1,0:T(8,128)}, pred[8,1,2,64,64]{4,3,2,1,0:T(32,1...) while((s32[]{:T(128)}, ...), condition=%wide.region_5.6_spmd.clone, body=%wide.region_3.5_spmd.clone.sunk | while | flops 227402880 | bytes 5011786 | solution.py:120
  616.1 18.2 all-gather.2
  651.0 39.4 %all-gather.24.cloned.1.call-done = bf16[1024,704]{0,1:T(8,128)(2,1)} async-done(((bf16[128,704]{0,1:T(8,128)(2,1)}), bf16[1024,704]{0,1:T(8,128)(2,1)}) %all-gather.24.cloned.1.call-update) | async-done | bytes 1441808 | tf_op jit(solution)/shard_map/all_gather | solution.py:212
  690.4 17.0 all-gather.22.cloned.1.call-done
  711.1 41.3 %all-gather.26.cloned.1.call-done = bf16[1024,704]{0,1:T(8,128)(2,1)} async-done(((bf16[128,704]{0,1:T(8,128)(2,1)}), bf16[1024,704]{0,1:T(8,128)(2,1)}) %all-gather.26.cloned.1.call-update) | async-done | bytes 1441808 | tf_op jit(solution)/shard_map/all_gather | solution.py:213
  768.9 44.9 %all-gather.28.cloned.1.call-done = bf16[704,1024]{1,0:T(8,128)(2,1)} async-done(((bf16[704,128]{1,0:T(8,128)(2,1)}), bf16[704,1024]{1,0:T(8,128)(2,1)}) %all-gather.28.cloned.1.call-update) | async-done | bytes 1441808 | tf_op jit(solution)/shard_map/all_gather | solution.py:214
  823.2 29.4 %reduce-scatter.35.cloned.1.call-done = f32[128,1024]{1,0:T(8,128)} async-done(((f32[512,1024]{1,0:T(8,128)}), f32[128,1024]{1,0:T(8,128)}) %reduce-scatter.35.cloned.1.call-update) | async-done | bytes 524304 | tf_op jit(solution)/shard_map/reduce_scatter | solution.py:306
  889.7 408.8 %while.92 = (s32[]{:T(128)}, f32[1,2,128,256]{2,3,1,0:T(8,128)S(1)}, f32[8,1,2,64,128]{4,3,2,1,0:T(8,128)}, f32[8,1,2,64,128]{4,3,0,2,1:T(8,128)}, f32[8,1,2,64,...) while((s32[]{:T(128)}, ...), condition=%wide.region_23.24_spmd.clone, body=%wide.region_13.23_spmd.clone.sunk | while | flops 460787776 | bytes 9353336 | solution.py:120
  1379.0 18.0 reduce-scatter.65.cloned.1.call-done
  1398.3 63.4 %reduce-scatter.61.cloned.1.call-done = f32[16,8]{1,0:T(8,128)} async-done(((f32[128,8]{1,0:T(8,128)}), f32[16,8]{1,0:T(8,128)}) %reduce-scatter.61.cloned.1.call-update) | async-done | bytes 528
  1463.3 63.3 %reduce-scatter.59.cloned.1.call-done = f32[16,8]{1,0:T(8,128)} async-done(((f32[128,8]{1,0:T(8,128)}), f32[16,8]{1,0:T(8,128)}) %reduce-scatter.59.cloned.1.call-update) | async-done | bytes 528
  1528.0 63.2 %reduce-scatter.63.cloned.1.call-done = f32[32,8]{1,0:T(8,128)} async-done(((f32[256,8]{1,0:T(8,128)}), f32[32,8]{1,0:T(8,128)}) %reduce-scatter.63.cloned.1.call-update) | async-done | bytes 1040
  1592.7 63.4 %reduce-scatter.57.cloned.1.call-done = f32[128,2]{1,0:T(8,128)} async-done(((f32[1024,2]{1,0:T(8,128)}), f32[128,2]{1,0:T(8,128)}) %reduce-scatter.57.cloned.1.call-update) | async-done | bytes 1040
  1657.5 63.3 %reduce-scatter.55.cloned.1.call-done = f32[128,2]{1,0:T(8,128)} async-done(((f32[1024,2]{1,0:T(8,128)}), f32[128,2]{1,0:T(8,128)}) %reduce-scatter.55.cloned.1.call-update) | async-done | bytes 1040
  1722.3 24.9 %reduce-scatter.37.cloned.1.call-done = bf16[128,1024]{1,0:T(8,128)(2,1)} async-done(((bf16[512,1024]{1,0:T(8,128)(2,1)}), bf16[128,1024]{1,0:T(8,128)(2,1)}) %reduce-scatter.37.cloned.1.call-update) | async-done | bytes 262160 | tf_op jit(solution)/shard_map/reduce_scatter | solution.py:327
  1748.5 39.5 %all-reduce.34 = (f32[1024]{0:T(1024)S(1)}, f32[8]{0:T(128)S(1)}, f32[8]{0:T(128)S(1)}, f32[1024]{0:T(1024)S(1)}) all-reduce(f32[1024]{0:T(1024)S(1)} %get-tuple-element.1875, f32[8]{0:T(128)S(1)} %multiply_dynamic-update-slice_fusion.2, f32[8]{0:T(128)S(1)} %dynamic_update_slice.258, ...), channel_id=1, replica_groups=mesh['dp'=8,'tensor'=4] {'dp','tensor'}, use_global_device_ids=true, to_apply=%region_29.30 | all-reduce | flops 2064 | bytes 16512 | tf_op jit(solution)/shard_map/psum | solution.py:374
  1792.5 58.8 %reduce-scatter.49.cloned.1.call-done = f32[128,704]{0,1:T(8,128)} async-done(((f32[1024,704]{0,1:T(8,128)}), f32[128,704]{0,1:T(8,128)}) %reduce-scatter.49.cloned.1.call-update) | async-done | bytes 360464 | tf_op jit(solution)/shard_map/reduce_scatter | solution.py:361
  1851.3 76.3 %reduce-scatter.51.cloned.1.call-done = f32[128,704]{0,1:T(8,128)} async-done(((f32[1024,704]{0,1:T(8,128)}), f32[128,704]{0,1:T(8,128)}) %reduce-scatter.51.cloned.1.call-update) | async-done | bytes 360464 | tf_op jit(solution)/shard_map/reduce_scatter | solution.py:362
  1927.7 76.3 %reduce-scatter.53.cloned.1.call-done = f32[704,128]{1,0:T(8,128)} async-done(((f32[704,1024]{1,0:T(8,128)}), f32[704,128]{1,0:T(8,128)}) %reduce-scatter.53.cloned.1.call-update) | async-done | bytes 360464 | tf_op jit(solution)/shard_map/reduce_scatter | solution.py:363
  2004.0 67.2 %reduce-scatter.41.cloned.1.call-done = f32[128,256]{1,0:T(8,128)} async-done(((f32[1024,256]{1,0:T(8,128)}), f32[128,256]{1,0:T(8,128)}) %reduce-scatter.41.cloned.1.call-update) | async-done | bytes 131088 | tf_op jit(solution)/shard_map/reduce_scatter | solution.py:351
  2071.2 67.1 %reduce-scatter.39.cloned.1.call-done = f32[128,256]{1,0:T(8,128)} async-done(((f32[1024,256]{1,0:T(8,128)}), f32[128,256]{1,0:T(8,128)}) %reduce-scatter.39.cloned.1.call-update) | async-done | bytes 131088 | tf_op jit(solution)/shard_map/reduce_scatter | solution.py:350
  2138.3 71.8 %reduce-scatter.47.cloned.1.call-done = f32[512,128]{1,0:T(8,128)} async-done(((f32[512,1024]{1,0:T(8,128)}), f32[512,128]{1,0:T(8,128)}) %reduce-scatter.47.cloned.1.call-update) | async-done | bytes 262160 | tf_op jit(solution)/shard_map/reduce_scatter | solution.py:360
  2210.1 71.3 %reduce-scatter.43.cloned.1.call-done = f32[128,512]{1,0:T(8,128)} async-done(((f32[1024,512]{1,0:T(8,128)}), f32[128,512]{1,0:T(8,128)}) %reduce-scatter.43.cloned.1.call-update) | async-done | bytes 262160 | tf_op jit(solution)/shard_map/reduce_scatter | solution.py:352
  2281.4 71.7 %reduce-scatter.45.cloned.1.call-done = f32[128,512]{1,0:T(8,128)} async-done(((f32[1024,512]{1,0:T(8,128)}), f32[128,512]{1,0:T(8,128)}) %reduce-scatter.45.cloned.1.call-update) | async-done | bytes 262160 | tf_op jit(solution)/shard_map/reduce_scatter | solution.py:353
  (1113 shorter events, 974.0 us)
Async XLA Ops:
  7.2 239.5 %all-gather.14.cloned.1.call-start = ((), (), s32[]{:S(2)}) async-start(), calls=%async_computation.18 | async-start | bytes 1310720 | tf_op jit(solution)/shard_map/all_gather | solution.py:240
  32.7 228.4 %all-gather.16.cloned.1.call-start = ((), (), s32[]{:S(2)}) async-start(), calls=%async_computation.19 | async-start | bytes 1179648 | tf_op jit(solution)/shard_map/all_gather | solution.py:202
  33.4 574.8 %all-gather.18.cloned.1.call-start = ((), (), s32[]{:S(2)}) async-start(), calls=%async_computation.20 | async-start | bytes 1179648 | tf_op jit(solution)/shard_map/all_gather | solution.py:203
  34.1 577.8 %all-gather.20.cloned.1.call-start = ((), (), s32[]{:S(2)}) async-start(), calls=%async_computation.21 | async-start | bytes 1179648 | tf_op jit(solution)/shard_map/all_gather | solution.py:210
  34.7 610.8 %reduce-scatter.31.cloned.1.call-start = ((), (), s32[]{:S(2)}) async-start(), calls=%async_computation.22 | async-start | bytes 2621440 | tf_op jit(solution)/shard_map/reduce_scatter | solution.py:260
  615.5 74.9 %all-gather.24.cloned.1.call-start = ((), (), s32[]{:S(2)}) async-start(), calls=%async_computation.24 | async-start | bytes 1622016 | tf_op jit(solution)/shard_map/all_gather | solution.py:212
  616.1 91.4 %all-gather.22.cloned.1.call-start = ((), (), s32[]{:S(2)}) async-start(), calls=%async_computation.23 | async-start | bytes 1310720 | tf_op jit(solution)/shard_map/all_gather | solution.py:270
  648.3 104.1 %all-gather.26.cloned.1.call-start = ((), (), s32[]{:S(2)}) async-start(), calls=%async_computation.25 | async-start | bytes 1622016 | tf_op jit(solution)/shard_map/all_gather | solution.py:213
  649.1 119.9 %all-gather.30.cloned.1.call-start = ((), (), s32[]{:S(2)}) async-start(), calls=%async_computation.28 | async-start | bytes 1310720 | tf_op jit(solution)/shard_map/all_gather | solution.py:241
  649.8 164.0 %all-gather.28.cloned.1.call-start = ((), (), s32[]{:S(2)}) async-start(), calls=%async_computation.26 | async-start | bytes 1622016 | tf_op jit(solution)/shard_map/all_gather | solution.py:214
  650.4 202.2 %reduce-scatter.35.cloned.1.call-start = ((), (), s32[]{:S(2)}) async-start(), calls=%async_computation.29 | async-start | bytes 2621440 | tf_op jit(solution)/shard_map/reduce_scatter | solution.py:306
  823.2 50.5 %all-gather.32.cloned.1.call-start = ((), (), s32[]{:S(2)}) async-start(), calls=%async_computation.30 | async-start | bytes 1310720 | tf_op jit(solution)/shard_map/all_gather | solution.py:317
  856.8 540.2 %reduce-scatter.65.cloned.1.call-start = ((), (), s32[]{:S(2)}) async-start(), calls=%async_computation.45 | async-start | bytes 147456
  1334.9 126.9 %reduce-scatter.61.cloned.1.call-start = ((), (), s32[]{:S(2)}) async-start(), calls=%async_computation.43 | async-start | bytes 73728
  1337.6 188.9 %reduce-scatter.59.cloned.1.call-start = ((), (), s32[]{:S(2)}) async-start(), calls=%async_computation.42 | async-start | bytes 73728
  1340.4 250.8 %reduce-scatter.63.cloned.1.call-start = ((), (), s32[]{:S(2)}) async-start(), calls=%async_computation.44 | async-start | bytes 147456
  1344.8 311.2 %reduce-scatter.57.cloned.1.call-start = ((), (), s32[]{:S(2)}) async-start(), calls=%async_computation.41 | async-start | bytes 589824
  1346.2 374.7 %reduce-scatter.55.cloned.1.call-start = ((), (), s32[]{:S(2)}) async-start(), calls=%async_computation.40 | async-start | bytes 589824
  1347.5 399.7 %reduce-scatter.37.cloned.1.call-start = ((), (), s32[]{:S(2)}) async-start(), calls=%async_computation.31 | async-start | bytes 1310720 | tf_op jit(solution)/shard_map/reduce_scatter | solution.py:327
  1354.1 436.2 %reduce-scatter.33.cloned.1.call-start = ((), (), s32[]{:S(2)}) async-start(), calls=%async_computation.27 | async-start | bytes 1310720 | tf_op jit(solution)/shard_map/reduce_scatter | solution.py:274
  1357.9 493.4 %reduce-scatter.49.cloned.1.call-start = ((), (), s32[]{:S(2)}) async-start(), calls=%async_computation.37 | async-start | bytes 3244032 | tf_op jit(solution)/shard_map/reduce_scatter | solution.py:361
  1360.5 567.2 %reduce-scatter.51.cloned.1.call-start = ((), (), s32[]{:S(2)}) async-start(), calls=%async_computation.38 | async-start | bytes 3244032 | tf_op jit(solution)/shard_map/reduce_scatter | solution.py:362
  1364.1 639.8 %reduce-scatter.53.cloned.1.call-start = ((), (), s32[]{:S(2)}) async-start(), calls=%async_computation.39 | async-start | bytes 3244032 | tf_op jit(solution)/shard_map/reduce_scatter | solution.py:363
  1368.1 703.1 %reduce-scatter.41.cloned.1.call-start = ((), (), s32[]{:S(2)}) async-start(), calls=%async_computation.33 | async-start | bytes 1179648 | tf_op jit(solution)/shard_map/reduce_scatter | solution.py:351
  1370.5 767.7 %reduce-scatter.39.cloned.1.call-start = ((), (), s32[]{:S(2)}) async-start(), calls=%async_computation.32 | async-start | bytes 1179648 | tf_op jit(solution)/shard_map/reduce_scatter | solution.py:350
  1372.1 838.0 %reduce-scatter.47.cloned.1.call-start = ((), (), s32[]{:S(2)}) async-start(), calls=%async_computation.36 | async-start | bytes 2359296 | tf_op jit(solution)/shard_map/reduce_scatter | solution.py:360
  1374.2 907.2 %reduce-scatter.43.cloned.1.call-start = ((), (), s32[]{:S(2)}) async-start(), calls=%async_computation.34 | async-start | bytes 2359296 | tf_op jit(solution)/shard_map/reduce_scatter | solution.py:352
  1376.4 976.7 %reduce-scatter.45.cloned.1.call-start = ((), (), s32[]{:S(2)}) async-start(), calls=%async_computation.35 | async-start | bytes 2359296 | tf_op jit(solution)/shard_map/reduce_scatter | solution.py:353
  1378.5 411.8 %copy-start.6 = (f32[128,1024]{1,0:T(8,128)S(1)}, f32[128,1024]{1,0:T(8,128)}, u32[]{:S(2)}) copy-start(f32[128,1024]{1,0:T(8,128)} %copy-done.5) | copy-start | bytes 1572868
  1378.5 411.8 %copy-start.17 = (f32[128,1024]{1,0:T(8,128)S(1)}, f32[128,1024]{1,0:T(8,128)}, u32[]{:S(2)}) copy-start(f32[128,1024]{1,0:T(8,128)} %reduce-scatter.35.cloned.1.call-done) | copy-start | bytes 1572868
  1378.6 411.7 %copy-start.31 = (bf16[128,1024]{1,0:T(8,128)(2,1)S(1)}, bf16[128,1024]{1,0:T(8,128)(2,1)}, u32[]{:S(2)}) copy-start(bf16[128,1024]{1,0:T(8,128)(2,1)} %param.45) | copy-start | bytes 786436
  1378.6 411.7 %copy-start.96 = (f32[128]{0:T(128)S(1)}, f32[128]{0:T(128)}, u32[]{:S(2)}) copy-start(f32[128]{0:T(128)} %copy-done.95) | copy-start | bytes 1540
  (155 other events, 4999.0 us)
Sparse Core Ops, SparseCore 0:
  32.8 13.9 all-gather.13
  48.9 43.8 all-gather.15
  95.0 38.8 all-gather.17
  135.7 38.1 all-gather.19
  615.6 29.8 reduce-scatter.30
  647.4 42.9 all-gather.23
  692.5 14.8 all-gather.21
  709.5 42.9 all-gather.25
  754.0 14.8 all-gather.29
  770.8 42.9 all-gather.27
  823.3 29.3 reduce-scatter.34
  857.0 16.7 all-gather.31
  1335.0 61.8 reduce-scatter.64
  1400.2 61.5 reduce-scatter.60
  1465.0 61.4 reduce-scatter.58
  1530.3 60.8 reduce-scatter.62
  1594.4 61.6 reduce-scatter.56
  1659.3 61.5 reduce-scatter.54
  1723.4 23.7 reduce-scatter.36
  1749.6 24.7 reduce-scatter.32
  1778.5 72.7 reduce-scatter.48
  1855.5 72.1 reduce-scatter.50
  1931.8 72.1 reduce-scatter.52
  2007.8 63.3 reduce-scatter.40
  2075.2 63.0 reduce-scatter.38
  2142.2 67.8 reduce-scatter.46
  2214.1 67.3 reduce-scatter.42
  2285.5 67.5 reduce-scatter.44
where the time goes:
time: 2380 us; the launch traced here: 2360 us
  waiting for transfers between devices  1130 us (47%)
  matrix products  357 us (15%)
  other arithmetic  347 us (15%)
  blocking collectives  288 us (12%)
  local copies, waits for them, and re-layouts  214 us (9%)
    unnamed x34, waiting for transfers between devices  339 us
    another operation x72, other arithmetic, delta_block(): lax.linalg.triangular_solve(system, target, left_side=True, lower=True, u...  187 us
    reduce_scatter x1, waiting for transfers between devices, per_device(): lax.psum_scatter(fup_grad, 'dp', scatter_dimension=0, tiled=True)  76.3 us
    reduce_scatter x1, waiting for transfers between devices, per_device(): lax.psum_scatter(down_grad, 'dp', scatter_dimension=1, tiled=True)  76.3 us
    reduce_scatter x1, waiting for transfers between devices, per_device(): lax.psum_scatter(outweight_grad, 'dp', scatter_dimension=1, tiled=True)  71.8 us
    reduce_scatter x1, waiting for transfers between devices, per_device(): lax.psum_scatter(proj_grads[3], 'dp', scatter_dimension=0, tiled=True)  71.7 us
    reduce_scatter x1, waiting for transfers between devices, per_device(): lax.psum_scatter(proj_grads[2], 'dp', scatter_dimension=0, tiled=True)  71.3 us
    reduce_scatter x1, waiting for transfers between devices, per_device(): lax.psum_scatter(proj_grads[1], 'dp', scatter_dimension=0, tiled=True)  67.2 us
  transfers between devices with their start and end apart: 28, of which 23 were waited for; matrix products, arithmetic and copies ran while one was open for 18% of the time, Pallas kernels for 0%

commit v1 on v0

v1 whole, which is shorter than its diff:
```python
from functools import partial

import jax
import jax.numpy as jnp
from jax import lax
from jax.experimental import pallas as pl
from jax.experimental.pallas import tpu as pltpu
from jax.sharding import PartitionSpec as P

LEN = 512
CHUNK = 128
TAPS = 4
HALO = 8
SMALL = 128

eps_norm = 1e-06
eps_output = 1e-05
EXACT = lax.Precision.HIGHEST
THREE = lax.Precision.HIGH
f32 = jnp.float32
bf16 = jnp.bfloat16


def mm(left, right, precision=None):
    return lax.dot_general(
        left, right, (((1,), (0,)), ((), ())), precision=precision, preferred_element_type=f32
    )


def mm_nt(left, right, precision=None):
    return lax.dot_general(
        left, right, (((1,), (1,)), ((), ())), precision=precision, preferred_element_type=f32
    )


def mm_tn(left, right, precision=None):
    return lax.dot_general(
        left, right, (((0,), (0,)), ((), ())), precision=precision, preferred_element_type=f32
    )


def sigmoid(value):
    return 1.0 / (1.0 + jnp.exp(-value))


def softplus(value):
    return jnp.maximum(value, 0.0) + jnp.log1p(jnp.exp(-jnp.abs(value)))


def iotas(size):
    row = lax.broadcasted_iota(jnp.int32, (size, size), 0)
    col = lax.broadcasted_iota(jnp.int32, (size, size), 1)
    return row, col


def conv_taps(block, before, meta, taps):
    size = block.shape[0]
    joined = jnp.concatenate([before, block], axis=0)
    total = taps[0:1] * block
    shifted = []
    for offset in range(1, TAPS):
        moved = joined[HALO - offset : HALO - offset + size] * meta[:, offset : offset + 1]
        shifted.append(moved)
        total = total + taps[offset : offset + 1] * moved
    return total, shifted


def gates(small, head, heads, decay_log, decay_bias):
    pre_a = small[:, head : head + 1] + decay_bias[:, head : head + 1]
    beta = sigmoid(small[:, heads + head : heads + head + 1])
    rate = -jnp.exp(decay_log[:, head : head + 1])
    return pre_a, beta, rate, rate * softplus(pre_a)


def decays(logdecay, meta, seg_row, row, col):
    size = logdecay.shape[0]
    within = (meta[:, 0:1] == seg_row) & (row >= col)
    ones_below = (row >= col).astype(f32)
    cumul = mm(ones_below, jnp.broadcast_to(logdecay, (size, size)), EXACT)
    spread = cumul - cumul.T
    decay = jnp.where(within, jnp.exp(jnp.where(within, spread, 0.0)), 0.0)
    carried = jnp.where(meta[:, 4:5] > 0.0, jnp.exp(cumul), 0.0)
    stays = meta[:, 0:1] == seg_row[:, size - 1 : size]
    weight = jnp.where(stays, jnp.exp(jnp.where(stays, cumul[size - 1 : size] - cumul, 0.0)), 0.0)
    return within, decay, carried, weight


def unit_inverse(lowers, row, col, precision):
    size = lowers[0].shape[0]
    eye = (row == col).astype(f32)
    base = 8
    same = (row // base) == (col // base)
    inner = [jnp.where(same, lower, 0.0) for lower in lowers]
    second = [mm(item, item, precision) for item in inner]
    fourth = [mm(item, item, precision) for item in second]
    inverse = [eye - item for item in inner]
    inverse = [item + mm(item, power, precision) for item, power in zip(inverse, second)]
    inverse = [item + mm(item, power, precision) for item, power in zip(inverse, fourth)]
    while base < size:
        joined = ((row // (2 * base)) == (col // (2 * base))) & ((row // base) != (col // base))
        outer = [jnp.where(joined, lower, 0.0) for lower in lowers]
        step = [mm(item, part, precision) for item, part in zip(inverse, outer)]
        step = [mm(item, part, precision) for item, part in zip(step, inverse)]
        inverse = [item - part for item, part in zip(inverse, step)]
        base = 2 * base
    return inverse


def mixer_forward_kernel(
    heads,
    width_k,
    width_v,
    proj,
    meta_ref,
    seg_ref,
    taps_ref,
    scalars_ref,
    gain_ref,
    gated_ref,
    raw_ref,
    update_ref,
    inverse_ref,
    state_ref,
    state,
    tail,
):
    step = pl.program_id(0)
    size = proj.shape[0]
    mixed = heads * (2 * width_k + width_v)
    small_at = mixed + heads * width_v

    @pl.when(step == 0)
    def _():
        state[...] = jnp.zeros_like(state)
        tail[...] = jnp.zeros_like(tail)

    meta = meta_ref[...]
    seg_row = seg_ref[0:1, :]
    decay_log = scalars_ref[0:1, :]
    decay_bias = scalars_ref[1:2, :]
    small = proj[:, small_at : small_at + SMALL]
    row, col = iotas(size)
    total, _ = conv_taps(proj[:, :mixed], tail[...], meta, taps_ref[...])
    tail[...] = proj[size - HALO : size, :mixed]
    active = total * sigmoid(total)
    queries, keys, values, betas, carries, weights, scores, lowers = [], [], [], [], [], [], [], []
    for head in range(heads):
        query = active[:, head * width_k : (head + 1) * width_k]
        query = query * (
            lax.rsqrt(jnp.sum(query * query, axis=1, keepdims=True) + eps_norm) * width_k**-0.5
        )
        key_at = heads * width_k + head * width_k
        key = active[:, key_at : key_at + width_k]
        key = key * lax.rsqrt(jnp.sum(key * key, axis=1, keepdims=True) + eps_norm)
        value_at = 2 * heads * width_k + head * width_v
        value = active[:, value_at : value_at + width_v]
        _, beta, _, logdecay = gates(small, head, heads, decay_log, decay_bias)
        within, decay, carried, weight = decays(logdecay, meta, seg_row, row, col)
        lower = jnp.where(row > col, beta * decay * mm_nt(key, key, THREE), 0.0)
        queries.append(query)
        keys.append(key)
        values.append(value)
        betas.append(beta)
        carries.append(carried)
        weights.append(weight)
        scores.append(mm_nt(query, key, THREE) * decay)
        lowers.append(lower)
    inverses = unit_inverse(lowers, row, col, THREE)
    for head in range(heads):
        entry = state[head]
        carried = carries[head]
        wide = jnp.concatenate([carried] * (width_v // size), axis=1)
        known = mm(keys[head], entry, THREE)
        target = betas[head] * (values[head] - wide * known)
        update = mm(inverses[head], target, THREE)
        output = wide * mm(queries[head], entry, THREE) + mm(scores[head], update, THREE)
        state_ref[0, head] = entry
        inverse_ref[0, head] = inverses[head]
        state[head] = wide[size - 1 : size] * entry + mm_tn(
            weights[head] * keys[head], update, THREE
        )
        span = slice(head * width_v, (head + 1) * width_v)
        update_ref[:, span] = update
        raw_ref[:, span] = output
        scale = lax.rsqrt(jnp.mean(output * output, axis=1, keepdims=True) + eps_output)
        pre = proj[:, mixed + head * width_v : mixed + (head + 1) * width_v]
        gated = output * scale * gain_ref[0:1, span] * (pre * sigmoid(pre))
        gated_ref[:, span] = gated.astype(bf16)


def mixer_backward_kernel(
    heads,
    width_k,
    width_v,
    proj,
    before_ref,
    meta_ref,
    seg_ref,
    taps_ref,
    scalars_ref,
    gain_ref,
    d_gated_ref,
    raw_ref,
    update_ref,
    inverse_ref,
    state_ref,
    d_proj_ref,
    d_taps_ref,
    d_gain_ref,
    d_scalars_ref,
    d_state,
    ahead,
):
    step = pl.program_id(0)
    size = proj.shape[0]
    mixed = heads * (2 * width_k + width_v)
    small_at = mixed + heads * width_v

    @pl.when(step == 0)
    def _():
        d_state[...] = jnp.zeros_like(d_state)
        ahead[...] = jnp.zeros_like(ahead)
        d_taps_ref[...] = jnp.zeros_like(d_taps_ref)
        d_gain_ref[...] = jnp.zeros_like(d_gain_ref)
        d_scalars_ref[...] = jnp.zeros_like(d_scalars_ref)

    meta = meta_ref[...]
    seg_row = seg_ref[0:1, :]
    decay_log = scalars_ref[0:1, :]
    decay_bias = scalars_ref[1:2, :]
    taps = taps_ref[...]
    small = proj[:, small_at : small_at + SMALL]
    row, col = iotas(size)
    block = proj[:, :mixed]
    total, shifted = conv_taps(block, before_ref[:, :mixed], meta, taps)
    gate = sigmoid(total)
    active = total * gate
    lane = lax.broadcasted_iota(jnp.int32, (size, SMALL), 1)
    small_grad = jnp.zeros((size, SMALL), f32)
    d_query_parts, d_key_parts, d_value_parts = [], [], []
    for head in range(heads):
        span = slice(head * width_v, (head + 1) * width_v)
        query_raw = active[:, head * width_k : (head + 1) * width_k]
        query_scale = lax.rsqrt(jnp.sum(query_raw * query_raw, axis=1, keepdims=True) + eps_norm)
        query_unit = query_raw * query_scale
        query = query_unit * width_k**-0.5
        key_at = heads * width_k + head * width_k
        key_raw = active[:, key_at : key_at + width_k]
        key_scale = lax.rsqrt(jnp.sum(key_raw * key_raw, axis=1, keepdims=True) + eps_norm)
        key = key_raw * key_scale
        value_at = 2 * heads * width_k + head * width_v
        value = active[:, value_at : value_at + width_v]
        pre_a, beta, rate, logdecay = gates(small, head, heads, decay_log, decay_bias)
        within, decay, carried, weight = decays(logdecay, meta, seg_row, row, col)
        wide = jnp.concatenate([carried] * (width_v // size), axis=1)
        keyed = decay * mm_nt(key, key, THREE)
        keyed = jnp.where(row > col, keyed, 0.0)
        scores = mm_nt(query, key, THREE) * decay
        entry = state_ref[0, head]
        inverse = inverse_ref[0, head]
        update = update_ref[:, span]
        output = raw_ref[:, span]
        scale = lax.rsqrt(jnp.mean(output * output, axis=1, keepdims=True) + eps_output)
        normed = output * scale
        pre = proj[:, mixed + head * width_v : mixed + (head + 1) * width_v]
        pre_gate = sigmoid(pre)
        silu = pre * pre_gate
        gain = gain_ref[0:1, span]
        d_gated = d_gated_ref[:, span]
        gained = d_gated * normed
        d_gain_ref[0:1, span] += jnp.sum(gained * silu, axis=0, keepdims=True)
        d_pre = gained * gain * (pre_gate * (1.0 + pre * (1.0 - pre_gate)))
        d_proj_ref[:, mixed + head * width_v : mixed + (head + 1) * width_v] = d_pre.astype(bf16)
        d_normed = d_gated * gain * silu
        d_output = scale * (
            d_normed - normed * jnp.mean(d_normed * normed, axis=1, keepdims=True)
        )
        d_exit = d_state[head]
        weighted = weight * key
        d_update = mm_tn(scores, d_output, THREE) + mm(weighted, d_exit, THREE)
        d_target = mm_tn(inverse, d_update, THREE)
        d_lower = jnp.where(row > col, -mm_nt(d_target, update, THREE), 0.0)
        d_scores = mm_nt(d_output, update, THREE)
        from_output = mm_nt(d_output, entry, THREE)
        from_target = mm_nt(d_target, entry, THREE)
        from_exit = mm_nt(update, d_exit, THREE)
        d_inner = d_scores * decay
        pair = d_lower * beta * decay
        d_query = carried * from_output + mm(d_inner, key, THREE)
        d_key = (
            mm_tn(d_inner, query, THREE)
            + weight * from_exit
            + mm(pair + pair.T, key, THREE)
            - beta * carried * from_target
        )
        d_value = beta * d_target
        d_state[head] = (
            wide[size - 1 : size] * d_exit
            + mm_tn(query, wide * d_output, THREE)
            - mm_tn(key, wide * d_value, THREE)
        )
        known_part = jnp.sum(key * from_target, axis=1, keepdims=True)
        carried_col = carried[:, 0:1]
        d_beta = (
            jnp.sum(d_target * value, axis=1, keepdims=True)
            - carried_col * known_part
            + jnp.sum(d_lower * keyed, axis=1, keepdims=True)
        )
        d_carried = jnp.sum(query * from_output, axis=1, keepdims=True) - beta * known_part
        d_spread = d_scores * scores + d_lower * (beta * keyed)
        d_weight = jnp.sum(weighted * from_exit, axis=1, keepdims=True)
        last = (row[:, 0:1] == size - 1).astype(f32)
        at_last = jnp.sum(d_weight, axis=0, keepdims=True) + carried_col[
            size - 1 : size
        ] * jnp.sum(jnp.sum(d_exit * entry, axis=1, keepdims=True), axis=0, keepdims=True)
        d_cumul = (
            jnp.sum(d_spread - d_spread.T, axis=1, keepdims=True)
            + d_carried * carried_col
            - d_weight
            + last * at_last
        )
        ones_above = (row <= col).astype(f32)
        d_logdecay = mm(ones_above, jnp.broadcast_to(d_cumul, (size, size)), EXACT)[:, 0:1]
        d_alpha = d_logdecay * rate * sigmoid(pre_a)
        d_scalars_ref[0:1, head : head + 1] += jnp.sum(
            d_logdecay * logdecay, axis=0, keepdims=True
        )
        d_scalars_ref[1:2, head : head + 1] += jnp.sum(d_alpha, axis=0, keepdims=True)
        small_grad = jnp.where(lane == head, d_alpha, small_grad)
        small_grad = jnp.where(lane == heads + head, d_beta * beta * (1.0 - beta), small_grad)
        d_query = d_query * width_k**-0.5
        d_query_parts.append(
            query_scale
            * (d_query - query_unit * jnp.sum(d_query * query_unit, axis=1, keepdims=True))
        )
        d_key_parts.append(key_scale * (d_key - key * jnp.sum(d_key * key, axis=1, keepdims=True)))
        d_value_parts.append(d_value)
    d_proj_ref[:, small_at : small_at + SMALL] = small_grad.astype(bf16)
    d_active = jnp.concatenate(d_query_parts + d_key_parts + d_value_parts, axis=1)
    d_total = d_active * (gate * (1.0 + total * (1.0 - gate)))
    d_block = taps[0:1] * d_total
    d_taps_ref[0:1, :] += jnp.sum(d_total * block, axis=0, keepdims=True)
    for offset in range(1, TAPS):
        d_taps_ref[offset : offset + 1, :] += jnp.sum(
            d_total * shifted[offset - 1], axis=0, keepdims=True
        )
        masked = d_total * meta[:, offset : offset + 1]
        joined = jnp.concatenate([masked, ahead[offset]], axis=0)
        d_block = d_block + taps[offset : offset + 1] * joined[offset : offset + size]
        ahead[offset] = masked[:HALO]
    d_proj_ref[:, :mixed] = d_block.astype(bf16)


def mixer_forward(proj, meta, seg_rows, taps, scalars, gain, heads, width_k, width_v):
    length = proj.shape[0]
    chunks = length // CHUNK
    mixed = heads * (2 * width_k + width_v)
    whole = lambda shape: pl.BlockSpec(shape, lambda c: (0,) * len(shape))
    rows = lambda width: pl.BlockSpec((CHUNK, width), lambda c: (c, 0))
    block4 = lambda a, b: pl.BlockSpec((1, heads, a, b), lambda c: (c, 0, 0, 0))
    return pl.pallas_call(
        partial(mixer_forward_kernel, heads, width_k, width_v),
        grid=(chunks,),
        in_specs=[
            rows(proj.shape[1]),
            rows(SMALL),
            pl.BlockSpec((8, CHUNK), lambda c: (c, 0)),
            whole(taps.shape),
            whole(scalars.shape),
            whole(gain.shape),
        ],
        out_specs=[
            rows(heads * width_v),
            rows(heads * width_v),
            rows(heads * width_v),
            block4(CHUNK, CHUNK),
            block4(width_k, width_v),
        ],
        out_shape=[
            jax.ShapeDtypeStruct((length, heads * width_v), bf16),
            jax.ShapeDtypeStruct((length, heads * width_v), f32),
            jax.ShapeDtypeStruct((length, heads * width_v), f32),
            jax.ShapeDtypeStruct((chunks, heads, CHUNK, CHUNK), f32),
            jax.ShapeDtypeStruct((chunks, heads, width_k, width_v), f32),
        ],
        scratch_shapes=[
            pltpu.VMEM((heads, width_k, width_v), f32),
            pltpu.VMEM((HALO, mixed), f32),
        ],
        name="mixer_forward",
    )(proj, meta, seg_rows, taps, scalars, gain)


def mixer_backward(
    proj, meta, seg_rows, taps, scalars, gain, d_gated, saved, heads, width_k, width_v
):
    length = proj.shape[0]
    chunks = length // CHUNK
    mixed = heads * (2 * width_k + width_v)
    last = chunks - 1
    per = CHUNK // HALO
    whole = lambda shape: pl.BlockSpec(shape, lambda c: (0,) * len(shape))
    rows = lambda width: pl.BlockSpec((CHUNK, width), lambda c: (last - c, 0))
    block4 = lambda a, b: pl.BlockSpec((1, heads, a, b), lambda c: (last - c, 0, 0, 0))
    raw, update, inverse, state = saved
    return pl.pallas_call(
        partial(mixer_backward_kernel, heads, width_k, width_v),
        grid=(chunks,),
        in_specs=[
            rows(proj.shape[1]),
            pl.BlockSpec(
                (HALO, proj.shape[1]), lambda c: (jnp.maximum((last - c) * per - 1, 0), 0)
            ),
            rows(SMALL),
            pl.BlockSpec((8, CHUNK), lambda c: (last - c, 0)),
            whole(taps.shape),
            whole(scalars.shape),
            whole(gain.shape),
            rows(heads * width_v),
            rows(heads * width_v),
            rows(heads * width_v),
            block4(CHUNK, CHUNK),
            block4(width_k, width_v),
        ],
        out_specs=[
            rows(proj.shape[1]),
            whole((8, mixed)),
            whole((8, heads * width_v)),
            whole((8, SMALL)),
        ],
        out_shape=[
            jax.ShapeDtypeStruct(proj.shape, bf16),
            jax.ShapeDtypeStruct((8, mixed), f32),
            jax.ShapeDtypeStruct((8, heads * width_v), f32),
            jax.ShapeDtypeStruct((8, SMALL), f32),
        ],
        scratch_shapes=[
            pltpu.VMEM((heads, width_k, width_v), f32),
            pltpu.VMEM((TAPS, HALO, mixed), f32),
        ],
        name="mixer_backward",
    )(proj, proj, meta, seg_rows, taps, scalars, gain, d_gated, raw, update, inverse, state)


def segment_tables(segment):
    length = segment.shape[0]
    columns = [segment.astype(f32)]
    for offset in range(1, TAPS):
        earlier = jnp.concatenate([jnp.full((offset,), -1, jnp.int32), segment[: length - offset]])
        columns.append((segment == earlier).astype(f32))
    ends = segment.reshape(-1, CHUNK)[:, -1]
    ends = jnp.concatenate([jnp.full((1,), -1, jnp.int32), ends[:-1]])
    columns.append((segment == jnp.repeat(ends, CHUNK)).astype(f32))
    meta = jnp.stack(columns, axis=1)
    meta = jnp.pad(meta, ((0, 0), (0, SMALL - meta.shape[1])))
    seg_rows = jnp.repeat(segment.astype(f32).reshape(-1, 1, CHUNK), 8, axis=1).reshape(-1, CHUNK)
    return meta, seg_rows


def row_scale(values):
    return lax.rsqrt(jnp.mean(values * values, axis=-1, keepdims=True) + eps_norm)


def norm_back(grad, normed, scale):
    return scale * (grad - normed * jnp.mean(grad * normed, axis=-1, keepdims=True))


def swap_core(value, axis, size):
    return lax.ppermute(value, axis, [(i, i ^ 1) for i in range(size)])


def swap_chip(value, axis, size):
    return lax.ppermute(value, axis, [(i, i ^ 2) for i in range(size)])


def pick(stacked, index, dim):
    return lax.dynamic_index_in_dim(stacked, index, dim, keepdims=False)


def interleave(mine, other, index, dim):
    first = index == 0
    return jnp.stack([jnp.where(first, mine, other), jnp.where(first, other, mine)], axis=dim)


def gather_rows(block, axis, size, chip, core):
    over = swap_chip(block, axis, size)
    pair = interleave(block, over, chip, 0)
    other = swap_core(pair, axis, size)
    return interleave(pair, other, core, 1).reshape(size * block.shape[0], block.shape[1])


def core_sum(partial_rows, axis, size, core):
    rows = partial_rows.shape[0] // size
    parts = partial_rows.reshape(2, 2, rows, partial_rows.shape[1])
    return pick(parts, core, 1) + swap_core(pick(parts, 1 - core, 1), axis, size)


def reduce_half(partial_rows, axis, size, core):
    mine = core_sum(partial_rows, axis, size, core).astype(bf16)
    return mine.astype(f32) + swap_chip(mine, axis, size).astype(f32)


def reduce_own(partial_rows, axis, size, chip, core):
    mine = core_sum(partial_rows, axis, size, core)
    away = swap_chip(pick(mine, 1 - chip, 0).astype(bf16), axis, size)
    return pick(mine, chip, 0) + away.astype(f32)


def join_halves(half, axis, size, core):
    other = swap_core(half, axis, size)
    return interleave(half, other, core, 1).reshape(-1, half.shape[-1])


def per_device(
    tokens,
    segment_ids,
    norm_gain_mixer,
    query_weight,
    key_weight,
    value_weight,
    gate_weight,
    alpha_weight,
    beta_weight,
    conv_query,
    conv_key,
    conv_value,
    decay_log,
    decay_bias,
    output_gain,
    output_weight,
    norm_gain_ffn,
    ffn_gate,
    ffn_up,
    ffn_down,
    grad_block,
):
    n_dp = lax.axis_size("dp")
    n_t = lax.axis_size("tensor")
    place = lax.axis_index("tensor")
    chip, core = place // 2, place % 2
    rows, width = tokens.shape
    owned = query_weight.shape[0]
    heads = decay_log.shape[0]
    width_k = query_weight.shape[1] // heads
    width_v = value_weight.shape[1] // heads
    hidden_units = ffn_gate.shape[1]
    mixed = heads * (2 * width_k + width_v)
    inner = heads * width_v
    gather_weights = lambda block: lax.all_gather(block, "dp", axis=0, tiled=True)

    thin = [
        alpha_weight,
        beta_weight,
        norm_gain_mixer.reshape(owned, 1),
        norm_gain_ffn.reshape(owned, 1),
        conv_query.reshape(owned, -1),
        conv_key.reshape(owned, -1),
        conv_value.reshape(owned, -1),
        jnp.pad(output_gain.reshape(-1), (0, owned - output_gain.size)).reshape(owned, 1),
    ]
    thin = jnp.concatenate(thin, axis=1)
    thin = jnp.pad(thin, ((0, 0), (0, SMALL - thin.shape[1])))
    weights = gather_weights(
        jnp.concatenate([query_weight, key_weight, value_weight, gate_weight, thin], axis=1)
    )
    later = gather_weights(
        jnp.concatenate([ffn_gate, ffn_up, ffn_down.T, output_weight.T], axis=1)
    )
    gate_up = later[:, : 2 * hidden_units]
    down_t = later[:, 2 * hidden_units : 3 * hidden_units]
    out_t = later[:, 3 * hidden_units :]

    tokens_full = gather_rows(tokens, "tensor", n_t, chip, core)
    grad_full = gather_rows(grad_block, "tensor", n_t, chip, core)

    thin_t = weights[:, mixed + inner :].astype(f32).T
    gain_mix = thin_t[2 * heads : 2 * heads + 1]
    gain_ffn = thin_t[2 * heads + 1 : 2 * heads + 2]

    def taps_of(first, count, size):
        flat = thin_t[first : first + count].T
        return flat.reshape(n_dp, TAPS, heads, size // n_dp).transpose(1, 2, 0, 3).reshape(TAPS, -1)

    at = 2 * heads + 2
    taps = jnp.concatenate(
        [taps_of(at, 1, width_k), taps_of(at + 1, 1, width_k), taps_of(at + 2, 2, width_v)], axis=1
    )
    taps = jnp.pad(taps, ((0, 8 - TAPS), (0, 0)))
    out_gain = thin_t[at + 4].reshape(n_dp, owned)[:, : output_gain.size]
    out_gain = out_gain.reshape(n_dp, heads, width_v // n_dp).transpose(1, 0, 2).reshape(1, inner)
    out_gain = jnp.pad(out_gain, ((0, 7), (0, 0)))
    scalars = jnp.pad(jnp.stack([decay_log, decay_bias]), ((0, 6), (0, SMALL - heads)))
    meta, seg_rows = segment_tables(segment_ids)

    resid_in = tokens_full.astype(f32)
    mixer_norm = resid_in * row_scale(resid_in)
    mixer_in = (mixer_norm * gain_mix).astype(bf16)
    proj = mm(mixer_in, weights)
    sizes = (heads, width_k, width_v)
    out_gated, *saved = mixer_forward(proj, meta, seg_rows, taps, scalars, out_gain, *sizes)
    mixer_out = reduce_half(mm_nt(out_gated, out_t), "tensor", n_t, core)

    def half_of(full):
        return pick(full.reshape(2, 2, rows, width), core, 1)

    resid = half_of(tokens_full).astype(f32) + mixer_out
    ffn_rms = row_scale(resid)
    ffn_norm = resid * ffn_rms
    ffn_in = join_halves((ffn_norm * gain_ffn).astype(bf16), "tensor", n_t, core)

    pre = mm(ffn_in, gate_up)
    gate_pre, up_pre = pre[:, :hidden_units], pre[:, hidden_units:]
    sigma = jax.nn.sigmoid(gate_pre)
    silu = gate_pre * sigma
    hidden = (silu * up_pre).astype(bf16)
    d_hidden = mm(grad_full, down_t)
    d_gate = d_hidden * up_pre * sigma * (1.0 + gate_pre * (1.0 - sigma))
    d_pre = jnp.concatenate([d_gate.astype(bf16), (d_hidden * silu).astype(bf16)], axis=1)
    d_ffn_in = reduce_half(mm_nt(d_pre, gate_up), "tensor", n_t, core)
    d_resid = half_of(grad_full).astype(f32) + norm_back(d_ffn_in * gain_ffn, ffn_norm, ffn_rms)
    d_mix = join_halves(d_resid.astype(bf16), "tensor", n_t, core)
    ffn_out = reduce_own(mm_nt(hidden, down_t), "tensor", n_t, chip, core)
    block_output = (pick(resid, chip, 0) + ffn_out).astype(bf16)
    ffn_gain_part = jnp.sum(pick(d_ffn_in * ffn_norm, chip, 0), axis=0)

    def scatter(blocks):
        joined = jnp.concatenate([block.astype(bf16) for block in blocks], axis=1)
        return lax.psum_scatter(joined, "dp", scatter_dimension=0, tiled=True).astype(f32)

    ffn_grads = scatter([mm_tn(ffn_in, d_pre), mm_tn(grad_full, hidden)])

    d_gated = mm(d_mix, out_t)
    d_proj, d_taps, d_gain, d_scalars = mixer_backward(
        proj, meta, seg_rows, taps, scalars, out_gain, d_gated, saved, *sizes
    )
    mixer_grads = scatter([mm_tn(d_mix, out_gated), mm_tn(mixer_in, d_proj)])
    d_mixer_in = reduce_own(mm_nt(d_proj, weights), "tensor", n_t, chip, core)
    own_tokens = tokens.astype(f32)
    own_rms = row_scale(own_tokens)
    own_norm = own_tokens * own_rms
    mix_gain_part = jnp.sum(d_mixer_in * own_norm, axis=0)
    tokens_grad = pick(d_resid, chip, 0) + norm_back(d_mixer_in * gain_mix, own_norm, own_rms)

    gain_sums = lax.psum((mix_gain_part, ffn_gain_part), ("dp", "tensor"))
    head_sums = lax.psum((d_taps[:TAPS], d_gain[0], d_scalars[:2, :heads]), "dp")
    dp_place = lax.axis_index("dp")
    mix_gain_grad, ffn_gain_grad = (
        lax.dynamic_slice_in_dim(part, dp_place * owned, owned, 0) for part in gain_sums
    )

    def own_columns(part, size):
        split = part.reshape(-1, heads, n_dp, size // n_dp)
        return lax.dynamic_index_in_dim(split, dp_place, 2, keepdims=False)

    taps_grad, gain_grad, scalars_grad = head_sums
    key_at, value_at = heads * width_k, 2 * heads * width_k
    conv_grads = (
        own_columns(taps_grad[:, :key_at], width_k),
        own_columns(taps_grad[:, key_at:value_at], width_k),
        own_columns(taps_grad[:, value_at:], width_v),
    )
    projected = mixer_grads[:, inner:]
    return (
        block_output,
        tokens_grad,
        mix_gain_grad,
        projected[:, :key_at],
        projected[:, key_at:value_at],
        projected[:, value_at:mixed],
        projected[:, mixed : mixed + inner],
        projected[:, mixed + inner : mixed + inner + heads],
        projected[:, mixed + inner + heads : mixed + inner + 2 * heads],
        *conv_grads,
        scalars_grad[0],
        scalars_grad[1],
        own_columns(gain_grad.reshape(1, -1), width_v)[0],
        mixer_grads[:, :inner].T,
        ffn_gain_grad,
        ffn_grads[:, :hidden_units],
        ffn_grads[:, hidden_units : 2 * hidden_units],
        ffn_grads[:, 2 * hidden_units :].T,
    )


def solution(mesh):
    by_rows = P(("dp", "tensor"), None)
    tiled, turned = P("dp", "tensor"), P("tensor", "dp")
    conv = P(None, "tensor", "dp")
    weights_in = (tiled,) * 6
    return jax.shard_map(
        per_device,
        mesh=mesh,
        in_specs=(
            by_rows,
            P("dp"),
            P("dp"),
            *weights_in,
            conv,
            conv,
            conv,
            P("tensor"),
            P("tensor"),
            turned,
            turned,
            P("dp"),
            tiled,
            tiled,
            turned,
            by_rows,
        ),
        out_specs=(
            by_rows,
            by_rows,
            P("dp"),
            *weights_in,
            conv,
            conv,
            conv,
            P("tensor"),
            P("tensor"),
            turned,
            turned,
            P("dp"),
            tiled,
            tiled,
            turned,
        ),
        check_vma=False,
    )
```

time: 2380 us -> 413 us (0.17)
  waiting for transfers between devices: 1130 us -> 170 us
  matrix products: 357 us -> 37.9 us
  other arithmetic: 347 us -> 28.6 us
  blocking collectives: 288 us -> 72.5 us
  local copies, waits for them, and re-layouts: 214 us -> 40.4 us
  Pallas kernels: 0 us -> 36.4 us
    reduce_scatter x12 -> x2, waiting for transfers between devices: 626 us -> 14.6 us  [scatter(): lax.psum_scatter(joined, 'dp', scatter_dimension=0, tiled=True).astype(f32)]
    unnamed x34 -> x4, waiting for transfers between devices: 339 us -> 0.07 us
    dot_general x180 -> x12, matrix products: 309 us -> 37.9 us  [the longest x4 14.3 us: mm(): lax.dot_general(left, right, (((1,), (0,)), ((), ())), precision=precisio...]
    all_gather x10 -> x0, blocking collectives: 248 us -> none  [the longest x1 32.6 us: per_device(): lax.all_gather(key_weight, 'dp', axis=0, tiled=True)]
    another operation x109 -> x13, other arithmetic: 214 us -> 2.48 us  [the longest x11 1.8 us: interleave(): jnp.stack([jnp.where(first, mine, other), jnp.where(first, other, mine)],...]
    all_gather x10 -> x2, waiting for transfers between devices: 165 us -> 109 us  [per_device(): lax.all_gather(block, 'dp', axis=0, tiled=True)]
    reduce_sum x40 -> x2, other arithmetic: 53.1 us -> 1.39 us  [the longest x1 1.12 us: per_device(): ffn_gain_part = jnp.sum(pick(d_ffn_in * ffn_norm, chip, 0), axis=0)]
    ppermute x0 -> x14, waiting for transfers between devices: none -> 46.7 us  [the longest x6 36.4 us: swap_chip(): return lax.ppermute(value, axis, [(i, i ^ 2) for i in range(size)])]
  transfers between devices with their start and end apart: 28 -> 18, of which waited for: 23 -> 14; matrix products, arithmetic and copies ran while one was open for 18% -> 17% of each run, Pallas kernels for 0% -> 9%
where the time goes in v1:
time: 413 us; the launch traced here: 412 us
  waiting for transfers between devices  170 us (41%)
  blocking collectives  72.5 us (18%)
  local copies, waits for them, and re-layouts  40.4 us (10%)
  matrix products  37.9 us (9%)
  Pallas kernels  36.4 us (9%)
  other arithmetic  28.6 us (7%)
  between operations  14.3 us (3%)
  starting transfers between devices  11.2 us (3%)
    all_gather x2, waiting for transfers between devices, per_device(): lax.all_gather(block, 'dp', axis=0, tiled=True)  109 us
    psum x1, blocking collectives, per_device(): gain_sums = lax.psum((mix_gain_part, ffn_gain_part), ('dp', 'tensor'))  37.1 us
    ppermute x6, waiting for transfers between devices, swap_chip(): return lax.ppermute(value, axis, [(i, i ^ 2) for i in range(size)])  36.4 us
    psum x1, blocking collectives, per_device(): lax.psum((d_taps[:TAPS], d_gain[0], d_scalars[:2, :heads]), 'dp')  35.3 us
    pallas_call x1, Pallas kernels, mixer_backward(): pl.pallas_call(partial(mixer_backward_kernel, heads, width_k, width_v), g...  19.3 us
    pallas_call x1, Pallas kernels, mixer_forward(): pl.pallas_call(partial(mixer_forward_kernel, heads, width_k, width_v), gr...  17.1 us
    unnamed x53, local copies, waits for them, and re-layouts  15.1 us
    reduce_scatter x2, waiting for transfers between devices, scatter(): lax.psum_scatter(joined, 'dp', scatter_dimension=0, tiled=True).astype(f32)  14.6 us
  transfers between devices with their start and end apart: 18, of which 14 were waited for; matrix products, arithmetic and copies ran while one was open for 17% of the time, Pallas kernels for 9%

profile of v1, /device:TPU:0, one launch (start us, length us, event | category | flops | bytes accessed | tf_op | source)
XLA Modules:
  0.0 411.8 jit_solution(1100108658229107831)
XLA Ops:
  15.7 2.1 pad_maximum_fusion.9
  17.9 3.0 collective-permute-start
  21.3 6.0 %collective-permute-done = bf16[128,1024]{1,0:T(8,128)(2,1)S(1)} collective-permute-done((bf16[128,1024]{1,0:T(8,128)(2,1)S(1)}, bf16[128,1024]{1,0:T(8,128)(2,1)S(1)}, u32[]{:S(2)}, u32[]{:S(2)}) %collective-permute-start) | collective-permute-done | bytes 262176 | tf_op jit(solution)/shard_map/ppermute | solution.py:473
  31.4 50.2 %all-gather.3.cloned.1.call-done = bf16[1024,1664]{1,0:T(8,128)(2,1)} async-done(((bf16[128,1664]{1,0:T(8,128)(2,1)}), bf16[1024,1664]{1,0:T(8,128)(2,1)}) %all-gather.3.cloned.1.call-update) | async-done | bytes 3407888 | tf_op jit(solution)/shard_map/all_gather | solution.py:549
  86.4 1.8 fusion.5
  88.3 6.5 %fusion.49.proj.before_ref = f32[512,1664]{1,0:T(8,128)} fusion(bf16[512,1024]{1,0:T(8,128)(2,1)S(1)} %fusion.5, bf16[1024,1664]{1,0:T(8,128)(2,1)} %all-gather.3.cloned.1.call-done), kind=kOutput, calls=%fused_computation.148 | convolution fusion | flops 1744830464 | bytes 7864320 | tf_op jit(solution)/shard_map/dot_general | solution.py:25
  94.8 17.1 %mixer_forward.1 = (bf16[512,512]{1,0:T(8,128)(2,1)}, f32[512,512]{1,0:T(8,128)}, f32[512,512]{1,0:T(8,128)}, f32[4,2,128,128]{3,2,1,0:T(8,128)}, f32[4,2,128,256]{3,2,1,0:T(8,128)}) custom-call(f32[512,1664]{1,0:T(8,128)} %fusion.49.proj.before_ref, f32[512,128]{1,0:T(8,128)} %pad.28.meta_ref, f32[32,128]{1,0:T(8,128)} %broadcast_bitcast_fusion.seg_ref, ...), custom_call_target="tpu_custom_call" | custom-call | tf_op jit(solution)/shard_map/mixer_forward/pallas_call | solution.py:361
  111.9 58.9 %all-gather.5.cloned.1.call-done = bf16[1024,2624]{0,1:T(8,128)(2,1)} async-done(((bf16[128,2624]{0,1:T(8,128)(2,1)}), bf16[1024,2624]{0,1:T(8,128)(2,1)}) %all-gather.5.cloned.1.call-update) | async-done | bytes 5373968 | tf_op jit(solution)/shard_map/all_gather | solution.py:549
  170.7 2.1 fusion.16
  179.9 3.6 collective-permute-done.7
  184.6 9.5 %collective-permute-done.3 = bf16[2,128,1024]{2,1,0:T(8,128)(2,1)S(1)} collective-permute-done((bf16[2,128,1024]{2,1,0:T(8,128)(2,1)S(1)}, bf16[2,128,1024]{2,1,0:T(8,128)(2,1)S(1)}, u32[]{:S(2)}, u32[]{:S(2)}) %collective-permute-start.3) | collective-permute-done | bytes 524320 | tf_op jit(solution)/shard_map/ppermute | solution.py:473
  199.1 2.6 multiply_convert_fusion.1
  202.6 2.1 convolution_convert_fusion.2
  204.7 2.6 copy.170
  207.3 3.6 convolution_convert_fusion
  210.9 2.4 pad_maximum_fusion.1
  213.4 4.1 fusion
  217.7 2.6 collective-permute-done.9
  222.0 12.5 %collective-permute-done.10 = bf16[2,128,1024]{2,1,0:T(8,128)(2,1)S(1)} collective-permute-done((bf16[2,128,1024]{2,1,0:T(8,128)(2,1)S(1)}, bf16[2,128,1024]{2,1,0:T(8,128)(2,1)S(1)}, u32[]{:S(2)}, u32[]{:S(2)}) %collective-permute-start.10) | collective-permute-done | bytes 524320 | tf_op jit(solution)/shard_map/ppermute | solution.py:473
  237.2 1.9 collective-permute-done.11
  243.7 3.3 fusion.14.d_gated_ref
  247.0 19.3 %mixer_backward.1 = (bf16[512,1664]{1,0:T(8,128)(2,1)}, f32[8,1024]{1,0:T(8,128)}, f32[8,512]{1,0:T(8,128)}, f32[8,128]{1,0:T(8,128)}) custom-call(f32[512,1664]{1,0:T(8,128)} %fusion.49.proj.before_ref, f32[512,1664]{1,0:T(8,128)} %fusion.49.proj.before_ref, f32[512,128]{1,0:T(8,128)} %pad.28.meta_ref, f32[32,128]{1,0:T(8,128)} %broadcast_bitcast_fusion.seg_ref, ...), custom_call_target="tpu_custom_call" | custom-call | tf_op jit(solution)/shard_map/mixer_backward/pallas_call | solution.py:406
  266.3 3.9 convolution_convert_fusion.1
  270.3 2.5 pad_maximum_fusion
  273.9 2.4 fusion.9
  277.8 2.7 collective-permute-done.5
  284.5 3.5 fusion.50
  296.0 35.3 %all-reduce.9 = (f32[4,1024]{1,0:T(4,128)S(1)}, f32[2,2]{1,0:T(2,128)S(1)}, f32[1,2,8,32]{3,1,2,0:T(2,128)S(1)}) all-reduce(f32[4,1024]{1,0:T(4,128)S(1)} %slice.141, f32[2,2]{1,0:T(2,128)S(1)} %slice.145, f32[1,2,8,32]{3,1,2,0:T(2,128)S(1)} %copy.169), channel_id=1, replica_groups=mesh['dp'=8,'tensor'=4] {'dp'}, use_global_device_ids=true, to_apply=%region_8.9 | all-reduce | flops 4612 | bytes 36896 | tf_op jit(solution)/shard_map/psum | solution.py:645
  332.8 1.9 bitcast_add_fusion
  337.3 3.9 collective-permute-done.13
  341.5 37.1 %all-reduce.8 = (f32[1024]{0:T(1024)S(1)}, f32[1024]{0:T(1024)S(1)}) all-reduce(f32[1024]{0:T(1024)S(1)} %get-tuple-element.138, f32[1024]{0:T(1024)S(1)} %fusion.31), channel_id=1, replica_groups=mesh['dp'=8,'tensor'=4] {'dp','tensor'}, use_global_device_ids=true, to_apply=%region_6.7 | all-reduce | flops 2048 | bytes 16384 | tf_op jit(solution)/shard_map/psum | solution.py:644
  384.8 14.6 %reduce-scatter.3.cloned.1.call-done = bf16[128,2176]{1,0:T(8,128)(2,1)} async-done(((bf16[1024,2176]{1,0:T(8,128)(2,1)}), bf16[128,2176]{1,0:T(8,128)(2,1)}) %reduce-scatter.3.cloned.1.call-update) | async-done | bytes 557072 | tf_op jit(solution)/shard_map/reduce_scatter | solution.py:628
  (182 shorter events, 71.8 us)
Async XLA Ops:
  7.2 10.7 %copy-start.1 = (bf16[128,1024]{1,0:T(8,128)(2,1)S(1)}, bf16[128,1024]{1,0:T(8,128)(2,1)}, u32[]{:S(2)}) copy-start(bf16[128,1024]{1,0:T(8,128)(2,1)} %param.21) | copy-start | bytes 786436
  7.2 13.7 %copy-start.12 = (s32[512]{0:T(512)S(1)}, s32[512]{0:T(512)}, u32[]{:S(2)}) copy-start(s32[512]{0:T(512)} %param.22) | copy-start | bytes 6148
  7.2 74.4 %all-gather.3.cloned.1.call-start = ((), (), s32[]{:S(2)}) async-start(), calls=%async_computation.2 | async-start | bytes 3833856 | tf_op jit(solution)/shard_map/all_gather | solution.py:549
  15.7 155.1 %all-gather.5.cloned.1.call-start = ((), (), s32[]{:S(2)}) async-start(), calls=%async_computation.3 | async-start | bytes 6045696 | tf_op jit(solution)/shard_map/all_gather | solution.py:549
  17.8 10.5 %copy-start.15 = (f32[2]{0:T(128)S(1)}, f32[2]{0:T(128)}, u32[]{:S(2)}) copy-start(f32[2]{0:T(128)} %param.34) | copy-start | bytes 28
  17.8 10.5 %copy-start.16 = (f32[2]{0:T(128)S(1)}, f32[2]{0:T(128)}, u32[]{:S(2)}) copy-start(f32[2]{0:T(128)} %param.33) | copy-start | bytes 28
  17.8 363.0 %reduce-scatter.5.cloned.1.call-start = ((), (), s32[]{:S(2)}) async-start(), calls=%async_computation.5 | async-start | bytes 5013504 | tf_op jit(solution)/shard_map/reduce_scatter | solution.py:628
  17.9 9.3 %collective-permute-start = (bf16[128,1024]{1,0:T(8,128)(2,1)S(1)}, bf16[128,1024]{1,0:T(8,128)(2,1)S(1)}, u32[]{:S(2)}, u32[]{:S(2)}) collective-permute-start(bf16[128,1024]{1,0:T(8,128)(2,1)S(1)} %copy-done.1), channel_id=1, source_target_pairs={{0,2},{1,3},{2,0},{3,1},{4,6},{5,7},{6,4},{7,5},{8,10},{9,11},{10,... | collective-permute-start | bytes 786440 | tf_op jit(solution)/shard_map/ppermute | solution.py:473
  27.3 2.2 collective-permute-start.1
  88.2 6.5 %copy-start.7 = (bf16[512,1024]{1,0:T(8,128)(2,1)}, bf16[512,1024]{1,0:T(8,128)(2,1)S(1)}, u32[]{:S(2)}) copy-start(bf16[512,1024]{1,0:T(8,128)(2,1)S(1)} %fusion.5) | copy-start | bytes 3145732
  173.9 3.0 collective-permute-start.2
  173.9 9.5 %collective-permute-start.7 = (bf16[128,1024]{1,0:T(8,128)(2,1)}, bf16[128,1024]{1,0:T(8,128)(2,1)}, u32[]{:S(2)}, u32[]{:S(2)}) collective-permute-start(bf16[128,1024]{1,0:T(8,128)(2,1)} %param.41), channel_id=1, source_target_pairs={{0,2},{1,3},{2,0},{3,1},{4,6},{5,7},{6,4},{7,5},{8,10},{9,11},{10,... | collective-permute-start | bytes 786440 | tf_op jit(solution)/shard_map/ppermute | solution.py:473
  178.3 15.8 %collective-permute-start.3 = (bf16[2,128,1024]{2,1,0:T(8,128)(2,1)S(1)}, bf16[2,128,1024]{2,1,0:T(8,128)(2,1)S(1)}, u32[]{:S(2)}, u32[]{:S(2)}) collective-permute-start(bf16[2,128,1024]{2,1,0:T(8,128)(2,1)S(1)} %fusion.13), channel_id=1, source_target_pairs={{0,2},{1,3},{2,0},{3,1},{4,6},{5,7},{6,4},{7,5},{8,10},{9,11},{10,... | collective-permute-start | bytes 1572872 | tf_op jit(solution)/shard_map/ppermute | solution.py:473
  184.5 10.3 %collective-permute-start.8 = (bf16[2,128,1024]{2,1,0:T(8,128)(2,1)S(1)}, bf16[2,128,1024]{2,1,0:T(8,128)(2,1)S(1)}, u32[]{:S(2)}, u32[]{:S(2)}) collective-permute-start(bf16[2,128,1024]{2,1,0:T(8,128)(2,1)S(1)} %pad_maximum_fusion.11), channel_id=1, source_target_pairs={{0,1},{1,0},{2,3},{3,2},{4,5},{5,4},{6,7},{7,6},{8,9},{9,8},{10,11... | collective-permute-start | bytes 1572872 | tf_op jit(solution)/shard_map/ppermute | solution.py:469
  194.6 2.5 slice-start
  194.8 2.0 collective-permute-start.4
  195.1 2.2 slice-start.1
  197.0 2.1 copy-start.8
  207.3 3.7 copy-start
  213.4 186.1 %reduce-scatter.3.cloned.1.call-start = ((), (), s32[]{:S(2)}) async-start(), calls=%async_computation.4 | async-start | bytes 5013504 | tf_op jit(solution)/shard_map/reduce_scatter | solution.py:628
  217.6 2.7 collective-permute-start.9
  220.5 14.0 %collective-permute-start.10 = (bf16[2,128,1024]{2,1,0:T(8,128)(2,1)S(1)}, bf16[2,128,1024]{2,1,0:T(8,128)(2,1)S(1)}, u32[]{:S(2)}, u32[]{:S(2)}) collective-permute-start(bf16[2,128,1024]{2,1,0:T(8,128)(2,1)S(1)} %fusion.12), channel_id=1, source_target_pairs={{0,2},{1,3},{2,0},{3,1},{4,6},{5,7},{6,4},{7,5},{8,10},{9,11},{10,... | collective-permute-start | bytes 1572872 | tf_op jit(solution)/shard_map/ppermute | solution.py:473
  237.2 1.9 collective-permute-start.11
  277.7 2.9 collective-permute-start.5
  277.8 6.7 %copy-start.13 = (bf16[1024,1664]{1,0:T(8,128)(2,1)S(1)}, bf16[1024,1664]{1,0:T(8,128)(2,1)}, u32[]{:S(2)}) copy-start(bf16[1024,1664]{1,0:T(8,128)(2,1)} %all-gather.3.cloned.1.call-done) | copy-start | bytes 10223620
  283.0 8.7 %collective-permute-start.6 = (bf16[128,1024]{1,0:T(8,128)(2,1)}, bf16[128,1024]{1,0:T(8,128)(2,1)}, u32[]{:S(2)}, u32[]{:S(2)}) collective-permute-start(bf16[128,1024]{1,0:T(8,128)(2,1)} %fusion.34), channel_id=1, source_target_pairs={{0,2},{1,3},{2,0},{3,1},{4,6},{5,7},{6,4},{7,5},{8,10},{9,11},{10,... | collective-permute-start | bytes 786440 | tf_op jit(solution)/shard_map/ppermute | solution.py:473
  289.4 5.1 %copy-start.14 = (f32[8,1024]{1,0:T(8,128)S(1)}, f32[8,1024]{1,0:T(8,128)}, u32[]{:S(2)}) copy-start(f32[8,1024]{1,0:T(8,128)} %get-tuple-element.35) | copy-start | bytes 98308
  290.5 42.4 %collective-permute-start.12 = (f32[2,128,1024]{2,1,0:T(8,128)}, f32[2,128,1024]{2,1,0:T(8,128)}, u32[]{:S(2)}, u32[]{:S(2)}) collective-permute-start(f32[2,128,1024]{2,1,0:T(8,128)} %dynamic-slice_bitcast_fusion), channel_id=1, source_target_pairs={{0,1},{1,0},{2,3},{3,2},{4,5},{5,4},{6,7},{7,6},{8,9},{9,8},{10,11... | collective-permute-start | bytes 3145736 | tf_op jit(solution)/shard_map/ppermute | solution.py:469
  332.8 46.9 %copy-start.4 = (f32[2,128,1024]{2,1,0:T(8,128)S(1)}, f32[2,128,1024]{2,1,0:T(8,128)}, u32[]{:S(2)}) copy-start(f32[2,128,1024]{2,1,0:T(8,128)} %get-tuple-element.151) | copy-start | bytes 3145732
  334.7 6.4 %collective-permute-start.13 = (bf16[128,1024]{1,0:T(8,128)(2,1)S(1)}, bf16[128,1024]{1,0:T(8,128)(2,1)S(1)}, u32[]{:S(2)}, u32[]{:S(2)}) collective-permute-start(bf16[128,1024]{1,0:T(8,128)(2,1)S(1)} %fusion.35), channel_id=1, source_target_pairs={{0,2},{1,3},{2,0},{3,1},{4,6},{5,7},{6,4},{7,5},{8,10},{9,11},{10,... | collective-permute-start | bytes 786440 | tf_op jit(solution)/shard_map/ppermute | solution.py:473
  380.8 3.0 copy-start.3
  399.4 4.3 %copy-start.2 = (bf16[128,2176]{1,0:T(8,128)(2,1)S(1)}, bf16[128,2176]{1,0:T(8,128)(2,1)}, u32[]{:S(2)}) copy-start(bf16[128,2176]{1,0:T(8,128)(2,1)} %reduce-scatter.3.cloned.1.call-done) | copy-start | bytes 1671172
  (7 other events, 7.6 us)
Sparse Core Ops, SparseCore 0:
  15.8 65.7 all-gather.2
  83.6 87.0 all-gather.4
  213.5 90.2 reduce-scatter.4
  307.3 92.0 reduce-scatter.2
